TPU v7x, 256 devices: a whole 4x4x8 slice. The times are simulated.
256 devices in a mesh: tm: 64 (over y, x, z_lo), agent: 4 (over z_hi, core).
Axes of the slice: x: 4, y: 4, z: 8 (z_hi: 2, z_lo: 4; z = z_hi * 4 + z_lo), core: 2. Of those that a mesh axis runs over, the one named last changes fastest.
Arguments:
- panel: bfloat16 [16384, 64, 128], P('tm', 'agent'), may hold values from -6 to 6
- w_tqkv: bfloat16 [128, 384], replicated, as said below
- w_tout: bfloat16 [128, 128], replicated, may hold values from -0.5 to 0.5
- w_cqkv: bfloat16 [128, 384], replicated, as said below
- w_cout: bfloat16 [128, 128], replicated, may hold values from -0.5 to 0.5
Outputs:
- block_out: bfloat16 [16384, 64, 128], P('tm', 'agent')
Inputs may be any that keep to these rules, and one draw needn't show every extreme that they name: `w_tqkv`: query, key and value weights with entries of order 128 ** -0.5, up to some tens of times that in query columns. `w_cqkv`: query, key and value weights with entries of order 128 ** -0.5, up to some tens of times that in query columns.
All inputs are finite; a program needn't handle non-finite values.
Results may differ from a plain program's by a relative error of at most 0.0045.
The roundings to bfloat16 on the way count: a program that leaves them out, or rounds other values in their place, can miss the bound.
Values may be sent and summed in bfloat16 or wider, within the bound.
A program may use at most 64 MiB of HBM per device.

v0:
```python
import math

import jax
import jax.numpy as jnp
from jax import lax
from jax.sharding import PartitionSpec as P

HEADS = 4
WINDOW = 256


epsilon = 1e-06


def shifted(value, axis, steps):
    count = lax.axis_size(axis)
    leading, last = (max(0, -steps), min(count, count - steps))
    return lax.ppermute(value, axis, [(source, source + steps) for source in range(leading, last)])


def normalize(values):
    widened = values.astype(jnp.float32)
    scale = lax.rsqrt(jnp.mean(widened * widened, axis=-1, keepdims=True) + epsilon)
    return (widened * scale).astype(jnp.bfloat16)


def project(normed, weight):
    shape = normed.shape
    result = jnp.dot(normed.reshape(-1, shape[-1]), weight, preferred_element_type=jnp.float32)
    return result.astype(jnp.bfloat16).reshape(shape[:-1] + (weight.shape[1],))


def softmax_rows(scores):
    top = jnp.max(scores, axis=-1, keepdims=True)
    expo = jnp.exp(scores - top)
    return (expo / jnp.sum(expo, axis=-1, keepdims=True)).astype(jnp.bfloat16)


def residual_add(base, attended, weight):
    update = jnp.dot(
        attended.reshape(-1, attended.shape[-1]), weight, preferred_element_type=jnp.float32
    )
    return (base.astype(jnp.float32) + update.reshape(base.shape)).astype(jnp.bfloat16)


def cross_block(qkv_rows):
    steps = qkv_rows.shape[0]
    count = qkv_rows.shape[1]
    width = qkv_rows.shape[2] // 3
    head_size = width // HEADS
    queries = qkv_rows[:, :, :width].reshape(steps, count, HEADS, head_size)
    keyset = qkv_rows[:, :, width : 2 * width].reshape(steps, count, HEADS, head_size)
    valset = qkv_rows[:, :, 2 * width :].reshape(steps, count, HEADS, head_size)
    scores = jnp.einsum(
        "tqhe,tkhe->thqk", queries, keyset, preferred_element_type=jnp.float32
    ) * head_size ** (-0.5)
    weights = softmax_rows(scores)
    attended = jnp.einsum("thqk,tkhe->tqhe", weights, valset, preferred_element_type=jnp.float32)
    return attended.astype(jnp.bfloat16).reshape(steps, count, width)


def local(panel, w_tqkv, w_tout, w_cqkv, w_cout):
    tm_dev, ag_dev, width = panel.shape
    head_size = width // HEADS
    normed_first = normalize(panel)
    qkv_first = project(normed_first, w_tqkv)
    queries = qkv_first[..., :width]
    own_pairs = qkv_first[..., width:]
    received = shifted(own_pairs, "tm", 1)
    key_rows = jnp.concatenate([received, own_pairs], 0)
    span = key_rows.shape[0]
    first_step = lax.axis_index("tm") * tm_dev
    rows_at = jnp.arange(tm_dev)[:, None]
    cols_at = jnp.arange(span)[None, :]
    allowed = (
        (cols_at - WINDOW <= rows_at) & (cols_at > rows_at) & (first_step + cols_at - WINDOW >= 0)
    )
    group_size = 8
    ngroups = ag_dev // group_size
    query_groups = queries.reshape(tm_dev, ngroups, group_size, HEADS, head_size).transpose(
        1, 0, 2, 3, 4
    )
    pair_groups = key_rows.reshape(span, ngroups, group_size, 2, HEADS, head_size).transpose(
        1, 0, 2, 3, 4, 5
    )

    def temporal_group(operands):
        group_queries, group_pairs = operands
        scores = jnp.einsum(
            "qahe,kahe->ahqk",
            group_queries,
            group_pairs[:, :, 0],
            preferred_element_type=jnp.float32,
        ) * head_size ** (-0.5)
        scores = jnp.where(allowed[None, None], scores, -jnp.inf)
        weights = softmax_rows(scores)
        attended = jnp.einsum(
            "ahqk,kahe->qahe", weights, group_pairs[:, :, 1], preferred_element_type=jnp.float32
        )
        return attended.astype(jnp.bfloat16)

    temporal_out = lax.map(temporal_group, (query_groups, pair_groups))
    temporal_out = temporal_out.transpose(1, 0, 2, 3, 4).reshape(tm_dev, ag_dev, width)
    mixed = residual_add(panel, temporal_out, w_tout)
    agent_count = lax.axis_size("agent")
    steps_each = tm_dev // agent_count
    blocks = mixed.reshape(agent_count, steps_each, ag_dev, width)
    slab = lax.all_to_all(blocks, "agent", split_axis=0, concat_axis=2, tiled=True)[0]
    nsteps = slab.shape[0]
    block_len = math.gcd(nsteps, 16)
    qkv_second = project(normalize(slab), w_cqkv)
    grouped = qkv_second.reshape((nsteps // block_len, block_len) + qkv_second.shape[1:])
    across = lax.map(cross_block, grouped).reshape(slab.shape)
    result = residual_add(slab, across, w_cout)
    restored = lax.all_to_all(result[None], "agent", split_axis=2, concat_axis=0, tiled=True)
    return restored.reshape(tm_dev, ag_dev, width)


def solution(mesh):
    in_specs = (P("tm", "agent", None), P(), P(), P(), P())
    out_specs = P("tm", "agent", None)
    return jax.shard_map(local, mesh=mesh, in_specs=in_specs, out_specs=out_specs, check_vma=False)
```

profile of v0, /device:TPU:33, one launch (start us, length us, event | category | flops | bytes accessed | tf_op | source)
XLA Modules:
  0.0 218.6 jit_solution(3051908601335071441)
XLA Ops:
  0.0 1.9 fusion.36
  1.9 1.7 fusion.37
  4.3 1.0 convolution_convert_fusion.2
  5.3 1.5 slice.30
  6.8 4.3 %copy.72 = bf16[256,16,256]{0,2,1:T(8,128)(2,1)} copy(bf16[256,16,256]{2,1,0:T(8,128)(2,1)} %slice.30) | data formatting | bytes 4194304
  11.1 3.5 %collective-permute-start = (bf16[256,16,256]{0,2,1:T(8,128)(2,1)}, bf16[256,16,256]{0,2,1:T(8,128)(2,1)}, u32[]{:S(2)}, u32[]{:S(2)}) collective-permute-start(bf16[256,16,256]{0,2,1:T(8,128)(2,1)} %copy.72), channel_id=1, source_target_pairs={{0,4},{4,8},{8,12},{12,16},{16,20},{20,24},{24,28},{28,32},{32,36}... | collective-permute-start | bytes 6291464 | tf_op jit(solution)/shard_map/ppermute | solution.py:18
  14.7 1.2 slice.31
  15.8 2.6 %copy.56 = bf16[256,16,128]{0,2,1:T(8,128)(2,1)} copy(bf16[256,16,128]{2,1,0:T(8,128)(2,1)} %slice.31) | data formatting | bytes 2097152 | tf_op jit(solution)/shard_map/slice | solution.py:67
  18.4 41.4 %collective-permute-done = bf16[256,16,256]{0,2,1:T(8,128)(2,1)} collective-permute-done((bf16[256,16,256]{0,2,1:T(8,128)(2,1)}, bf16[256,16,256]{0,2,1:T(8,128)(2,1)}, u32[]{:S(2)}, u32[]{:S(2)}) %collective-permute-start) | collective-permute-done | bytes 2097184 | tf_op jit(solution)/shard_map/ppermute | solution.py:18
  59.8 3.9 %pad_maximum_fusion = bf16[512,16,256]{0,2,1:T(8,128)(2,1)} fusion(bf16[256,16,256]{0,2,1:T(8,128)(2,1)S(1)} %copy-done.3, bf16[256,16,256]{0,2,1:T(8,128)(2,1)} %collective-permute-done), kind=kLoop, calls=%fused_computation.44 | loop fusion | flops 8388608 | bytes 8388608 | tf_op jit(solution)/shard_map/concatenate | solution.py:70
  63.7 40.0 %while.22 = (s32[]{:T(128)}, bf16[2,256,8,4,32]{1,4,3,2,0:T(8,128)(2,1)}, bf16[2,512,8,2,4,32]{1,5,4,3,2,0:T(8,128)(2,1)}, bf16[2,256,8,4,32]{1,4,3,2,0:T(8,128)...) while((s32[]{:T(128)}, bf16[2,256,8,4,32]{1,4,3,2,0:T(8,128)(2,1)}, ...), condition=%wide.region_4.5_spmd.clone, body=%wide.region_1.4_spmd.clone.sunk | while | flops 562823680 | bytes 41226316 | solution.py:102
  63.7 1.8 copy_bitcast_fusion.2
  65.6 10.2 %fusion.76 = (f32[8,4,256]{2,1,0:T(4,128)S(1)}, f32[8,4,256,512]{3,2,1,0:T(8,128)}) fusion(pred[256,512]{1,0:T(8,128)(4,1)S(1)} %fusion.75, bf16[512,8,2,4,32]{0,4,3,1,2:T(8,128)(2,1)S(1)} %copy_bitcast_fusion.2, bf16[2,256,8,4,32]{1,4,3,2,0:T(8,128)(2,1)} %get-tuple-element.218, s32[]{:T(128)} %get-tuple-element.208), kind=kOutput, calls=%fused_computation.66.clone.1 | convolution fusion | flops 285213184 | bytes 18514432 | tf_op jit(solution)/shard_map/while/body/eval_jaxpr/sub | solution.py:35
  75.8 7.9 %fusion.77 = bf16[2,256,8,4,32]{1,4,3,2,0:T(8,128)(2,1)} fusion(bf16[2,256,8,4,32]{1,4,3,2,0:T(8,128)(2,1)} %get-tuple-element.209, s32[]{:T(128)} %get-tuple-element.208, f32[8,4,256,512]{3,2,1,0:T(8,128)} %get-tuple-element.199, f32[8,4,256]{2,1,0:T(4,128)S(1)} %get-tuple-element.200, bf16[512,8,2,4,32]{0,4,3,1,2:T(8,128)(2,1)S(1)} %copy_bitcast_fusion.2), kind=kOutput, calls=%fused_computation.25.clone.1 | convolution fusion | flops 277086208 | bytes 18383360 | tf_op jit(solution)/shard_map/while/body/eval_jaxpr/ahqk,kahe->qahe/dot_general | solution.py:97
  83.7 1.7 copy_bitcast_fusion.2
  85.6 10.2 %fusion.76 = (f32[8,4,256]{2,1,0:T(4,128)S(1)}, f32[8,4,256,512]{3,2,1,0:T(8,128)}) fusion(pred[256,512]{1,0:T(8,128)(4,1)S(1)} %fusion.75, bf16[512,8,2,4,32]{0,4,3,1,2:T(8,128)(2,1)S(1)} %copy_bitcast_fusion.2, bf16[2,256,8,4,32]{1,4,3,2,0:T(8,128)(2,1)} %get-tuple-element.218, s32[]{:T(128)} %get-tuple-element.208), kind=kOutput, calls=%fused_computation.66.clone.1 | convolution fusion | flops 285213184 | bytes 18514432 | tf_op jit(solution)/shard_map/while/body/eval_jaxpr/sub | solution.py:35
  95.7 7.9 %fusion.77 = bf16[2,256,8,4,32]{1,4,3,2,0:T(8,128)(2,1)} fusion(bf16[2,256,8,4,32]{1,4,3,2,0:T(8,128)(2,1)} %get-tuple-element.209, s32[]{:T(128)} %get-tuple-element.208, f32[8,4,256,512]{3,2,1,0:T(8,128)} %get-tuple-element.199, f32[8,4,256]{2,1,0:T(4,128)S(1)} %get-tuple-element.200, bf16[512,8,2,4,32]{0,4,3,1,2:T(8,128)(2,1)S(1)} %copy_bitcast_fusion.2), kind=kOutput, calls=%fused_computation.25.clone.1 | convolution fusion | flops 277086208 | bytes 18383360 | tf_op jit(solution)/shard_map/while/body/eval_jaxpr/ahqk,kahe->qahe/dot_general | solution.py:97
  103.7 1.8 fusion.38
  105.5 1.7 copy.59
  107.1 9.1 %all-to-all-start = ((bf16[4,64,16,128]{3,2,1,0:T(8,128)(2,1)}), bf16[4,64,16,128]{3,2,1,0:T(8,128)(2,1)S(1)}, u32[]{:S(2)}, u32[]{:S(2)}) async-start(bf16[4,64,16,128]{3,2,1,0:T(8,128)(2,1)} %copy.59), calls=%async_computation | async-start | bytes 2097152 | tf_op jit(solution)/shard_map/all_to_all | solution.py:108
  116.2 28.7 %all-to-all-done = bf16[4,64,16,128]{3,2,1,0:T(8,128)(2,1)S(1)} async-done(((bf16[4,64,16,128]{3,2,1,0:T(8,128)(2,1)}), bf16[4,64,16,128]{3,2,1,0:T(8,128)(2,1)S(1)}, u32[]{:S(2)}, u32[]{:S(2)}) %all-to-all-start) | async-done | bytes 1048608 | tf_op jit(solution)/shard_map/all_to_all | solution.py:108
  146.3 1.4 copy-done.1
  147.6 0.8 fusion.39
  148.5 2.6 %convolution_convert_fusion.1 = bf16[4096,384]{1,0:T(8,128)(2,1)} fusion(bf16[4096,128]{1,0:T(8,128)(2,1)S(1)} %fusion.39, bf16[128,384]{1,0:T(8,128)(2,1)S(1)} %copy-done.4), kind=kOutput, calls=%fused_computation.42 | convolution fusion | flops 404226048 | bytes 4292608 | tf_op jit(solution)/shard_map/dot_general | solution.py:29
  151.1 29.8 %while.21 = (s32[]{:T(128)}, bf16[4,16,64,128]{2,3,1,0:T(8,128)(2,1)}, bf16[4,16,64,384]{3,2,1,0:T(8,128)(2,1)}, s32[]{:T(128)}) while((s32[]{:T(128)}, bf16[4,16,64,128]{2,3,1,0:T(8,128)(2,1)}, bf16[4,16,64,384]{3,2,1,0:T(8,128)(2,1)}, s32[]{:T(128)}) %tuple.60), condition=%wide.region_9.10_spmd, body=%wide.region_6.9_spmd.sunk | while | flops 34996288 | bytes 8684089 | solution.py:113
  151.2 1.2 constant_dynamic-slice_fusion.5
  152.4 0.9 copy.82
  153.4 2.3 %fusion.73 = (f32[16,4,64]{2,1,0:T(4,128)S(1)}, f32[16,4,64,64]{2,3,1,0:T(8,128)}) fusion(bf16[16,64,4,32]{1,3,2,0:T(8,128)(2,1)S(1)} %bitcast.127, bf16[16,64,4,32]{1,3,2,0:T(8,128)(2,1)S(1)} %bitcast.126), kind=kOutput, calls=%fused_computation.65.clone.1 | convolution fusion | flops 17563712 | bytes 1589248 | tf_op jit(solution)/shard_map/while/body/eval_jaxpr/sub | solution.py:35
  155.8 2.0 convolution_convert_fusion.4
  157.8 0.8 constant_dynamic-update-slice_fusion.2
  158.6 1.2 constant_dynamic-slice_fusion.5
  159.8 0.9 copy.82
  160.9 2.3 %fusion.73 = (f32[16,4,64]{2,1,0:T(4,128)S(1)}, f32[16,4,64,64]{2,3,1,0:T(8,128)}) fusion(bf16[16,64,4,32]{1,3,2,0:T(8,128)(2,1)S(1)} %bitcast.127, bf16[16,64,4,32]{1,3,2,0:T(8,128)(2,1)S(1)} %bitcast.126), kind=kOutput, calls=%fused_computation.65.clone.1 | convolution fusion | flops 17563712 | bytes 1589248 | tf_op jit(solution)/shard_map/while/body/eval_jaxpr/sub | solution.py:35
  163.2 2.0 convolution_convert_fusion.4
  165.2 0.9 constant_dynamic-update-slice_fusion.2
  166.1 1.2 constant_dynamic-slice_fusion.5
  167.3 0.9 copy.82
  168.3 2.3 %fusion.73 = (f32[16,4,64]{2,1,0:T(4,128)S(1)}, f32[16,4,64,64]{2,3,1,0:T(8,128)}) fusion(bf16[16,64,4,32]{1,3,2,0:T(8,128)(2,1)S(1)} %bitcast.127, bf16[16,64,4,32]{1,3,2,0:T(8,128)(2,1)S(1)} %bitcast.126), kind=kOutput, calls=%fused_computation.65.clone.1 | convolution fusion | flops 17563712 | bytes 1589248 | tf_op jit(solution)/shard_map/while/body/eval_jaxpr/sub | solution.py:35
  170.7 2.0 convolution_convert_fusion.4
  172.7 0.9 constant_dynamic-update-slice_fusion.2
  173.5 1.2 constant_dynamic-slice_fusion.5
  174.7 0.9 copy.82
  175.8 2.3 %fusion.73 = (f32[16,4,64]{2,1,0:T(4,128)S(1)}, f32[16,4,64,64]{2,3,1,0:T(8,128)}) fusion(bf16[16,64,4,32]{1,3,2,0:T(8,128)(2,1)S(1)} %bitcast.127, bf16[16,64,4,32]{1,3,2,0:T(8,128)(2,1)S(1)} %bitcast.126), kind=kOutput, calls=%fused_computation.65.clone.1 | convolution fusion | flops 17563712 | bytes 1589248 | tf_op jit(solution)/shard_map/while/body/eval_jaxpr/sub | solution.py:35
  178.1 2.0 convolution_convert_fusion.4
  180.1 0.9 constant_dynamic-update-slice_fusion.2
  181.0 2.9 %fusion.41 = bf16[1,64,64,128]{3,2,1,0:T(8,128)(2,1)S(1)} fusion(bf16[64,64,128]{1,2,0:T(8,128)(2,1)} %bitcast.131, f32[4,64,16,128]{3,2,0,1:T(8,128)} %copy-done.1, bf16[128,128]{1,0:T(8,128)(2,1)S(1)} %copy-done.6), kind=kOutput, calls=%fused_computation.56 | convolution fusion | flops 135266304 | bytes 4227072 | tf_op jit(solution)/shard_map/dot_general | solution.py:40
  184.6 32.3 %all_to_all.24 = bf16[1,64,64,128]{3,1,0,2:T(8,128)(2,1)S(1)} all-to-all(bf16[1,64,64,128]{3,1,0,2:T(8,128)(2,1)S(1)} %copy.65), channel_id=1, replica_groups=mesh['tm'=64,'agent'=4] {'agent'}, dimensions={2} | all-to-all | bytes 2097152 | tf_op jit(solution)/shard_map/all_to_all | solution.py:115
  216.9 1.6 copy.66
  (32 shorter events, 3.6 us)
Async XLA Ops:
  0.0 4.3 %copy-start = (bf16[128,384]{1,0:T(8,128)(2,1)S(1)}, bf16[128,384]{1,0:T(8,128)(2,1)}, u32[]{:S(2)}) copy-start(bf16[128,384]{1,0:T(8,128)(2,1)} %param.10) | copy-start | bytes 294916
  11.1 48.7 %collective-permute-start = (bf16[256,16,256]{0,2,1:T(8,128)(2,1)}, bf16[256,16,256]{0,2,1:T(8,128)(2,1)}, u32[]{:S(2)}, u32[]{:S(2)}) collective-permute-start(bf16[256,16,256]{0,2,1:T(8,128)(2,1)} %copy.72), channel_id=1, source_target_pairs={{0,4},{4,8},{8,12},{12,16},{16,20},{20,24},{24,28},{28,32},{32,36}... | collective-permute-start | bytes 6291464 | tf_op jit(solution)/shard_map/ppermute | solution.py:18
  15.8 44.0 %copy-start.3 = (bf16[256,16,256]{0,2,1:T(8,128)(2,1)S(1)}, bf16[256,16,256]{0,2,1:T(8,128)(2,1)}, u32[]{:S(2)}) copy-start(bf16[256,16,256]{0,2,1:T(8,128)(2,1)} %copy.72) | copy-start | bytes 6291460
  63.7 40.0 %copy-start.2 = (bf16[256,16,128]{2,1,0:T(8,128)(2,1)S(1)}, bf16[256,16,128]{2,1,0:T(8,128)(2,1)}, u32[]{:S(2)}) copy-start(bf16[256,16,128]{2,1,0:T(8,128)(2,1)} %param.9) | copy-start | bytes 3145732
  63.7 40.0 %copy-start.5 = (bf16[128,128]{1,0:T(8,128)(2,1)S(1)}, bf16[128,128]{1,0:T(8,128)(2,1)}, u32[]{:S(2)}) copy-start(bf16[128,128]{1,0:T(8,128)(2,1)} %param.11) | copy-start | bytes 98308
  107.1 37.8 %all-to-all-start = ((bf16[4,64,16,128]{3,2,1,0:T(8,128)(2,1)}), bf16[4,64,16,128]{3,2,1,0:T(8,128)(2,1)S(1)}, u32[]{:S(2)}, u32[]{:S(2)}) async-start(bf16[4,64,16,128]{3,2,1,0:T(8,128)(2,1)} %copy.59), calls=%async_computation | async-start | bytes 2097152 | tf_op jit(solution)/shard_map/all_to_all | solution.py:108
  146.2 1.4 copy-start.1
  147.6 0.9 copy-start.4
  151.1 29.8 %copy-start.6 = (bf16[128,128]{1,0:T(8,128)(2,1)S(1)}, bf16[128,128]{1,0:T(8,128)(2,1)}, u32[]{:S(2)}) copy-start(bf16[128,128]{1,0:T(8,128)(2,1)} %param.13) | copy-start | bytes 98308
where the time goes:
time: 220 us; the launch traced here: 219 us
  waiting for transfers between devices  70 us (32%)
  matrix products  61.7 us (28%)
  blocking collectives  32.3 us (15%)
  local copies, waits for them, and re-layouts  31.9 us (14%)
  starting transfers between devices  12.7 us (6%)
  other arithmetic  9.6 us (4%)
    ppermute x1, waiting for transfers between devices, shifted(): lax.ppermute(value, axis, [(source, source + steps) for source in range(l...  41.4 us
    all_to_all x1, blocking collectives, local(): lax.all_to_all(result[None], 'agent', split_axis=2, concat_axis=0, tiled=...  32.3 us
    sub x6, matrix products, softmax_rows(): expo = jnp.exp(scores - top)  29.7 us
    all_to_all x1, waiting for transfers between devices, local(): lax.all_to_all(blocks, 'agent', split_axis=0, concat_axis=2, tiled=True)[0]  28.7 us
    dot_general x2, matrix products, temporal_group(): jnp.einsum('ahqk,kahe->qahe', weights, group_pairs[:, :, 1], preferred_el...  15.9 us
    all_to_all x1, starting transfers between devices, local(): lax.all_to_all(blocks, 'agent', split_axis=0, concat_axis=2, tiled=True)[0]  9.12 us
    dynamic_slice x8, local copies, waits for them, and re-layouts, local(): across = lax.map(cross_block, grouped).reshape(slab.shape)  8.39 us
    dot_general x4, matrix products, cross_block(): jnp.einsum('thqk,tkhe->tqhe', weights, valset, preferred_element_type=jnp...  7.92 us
  transfers between devices with their start and end apart: 2, of which 2 were waited for; matrix products, arithmetic and copies ran while one was open for 2% of the time, Pallas kernels for 0%

commit v1 on v0

v1 whole, which is shorter than its diff:
```python
import functools
import math

import jax
import jax.numpy as jnp
from jax import lax
from jax.experimental import pallas as pl
from jax.experimental.pallas import tpu as pltpu
from jax.sharding import PartitionSpec as P

HEADS = 4
WINDOW = 256
EPSILON = 1e-06
UNROLL = 4
PARTS = 2
BLOCK = 4
BLOCKS = 2
MESH = pl.DeviceIdType.MESH
NT = (((1,), (1,)), ((), ()))
NN = (((1,), (0,)), ((), ()))


def matmul(left, right, dims=NN):
    return lax.dot_general(left, right, dims, preferred_element_type=jnp.float32)


def normalized(values):
    widened = values.astype(jnp.float32)
    scale = lax.rsqrt(jnp.mean(widened * widened, axis=-1, keepdims=True) + EPSILON)
    return (widened * scale).astype(jnp.bfloat16)


def by_head(values, masks):
    return jnp.concatenate([values * mask for mask in masks], axis=0)


def pick_heads(stacked, rows, picks):
    blocks = [stacked[h * rows : (h + 1) * rows] for h in range(HEADS)]
    result = blocks[-1]
    for pick, block in zip(picks, blocks):
        result = jnp.where(pick, block, result)
    return result


def kernel(
    x_hbm, wt_hbm, wto_hbm, wc_hbm, wco_hbm, out_hbm,
    xv, halo, wt, wto, wc, wco, wide, q1, k1, v1, upd, mixed, slab, wvt, own_out, sib_out,
    load_sem, halo_send, halo_recv, mix_send, mix_recv, res_send, res_recv, store_sem,
    *, tm_axis, agent_axis, chunk,
):
    tm_dev, ag_dev, width = xv.shape
    chunks = tm_dev // chunk
    half = chunk // 2
    part = half // PARTS
    pieces = chunks * PARTS
    agents = slab.shape[1]
    pair = 2 * ag_dev
    head_size = width // HEADS
    factor = math.log2(math.e) * head_size ** (-0.5)
    tm = lax.axis_index(tm_axis)
    ag = lax.axis_index(agent_axis)
    tm_count = lax.axis_size(tm_axis)
    side = ag // 2
    core = ag % 2
    ahead = (lax.rem(tm + 1, tm_count), ag)
    behind = (lax.rem(tm + tm_count - 1, tm_count), ag)
    sibling = (tm, side * 2 + 1 - core)
    far = [(tm, (1 - side) * 2 + j) for j in range(2)]

    loads = [
        pltpu.make_async_copy(src, dst, load_sem.at[i])
        for i, (src, dst) in enumerate(
            [(x_hbm, xv), (wt_hbm, wt), (wto_hbm, wto), (wc_hbm, wc), (wco_hbm, wco)]
        )
    ]
    for load in loads:
        load.start()

    barrier = pltpu.get_barrier_semaphore()
    for peer in (ahead, behind, sibling, far[0], far[1]):
        pl.semaphore_signal(barrier, inc=1, device_id=peer, device_id_type=MESH)
    pl.semaphore_wait(barrier, 5)

    def halo_copy(c):
        rows = pl.ds(c * chunk, chunk)
        return pltpu.make_async_remote_copy(
            src_ref=x_hbm.at[rows], dst_ref=halo.at[rows],
            send_sem=halo_send.at[c], recv_sem=halo_recv.at[c],
            device_id=ahead, device_id_type=MESH,
        )

    for c in reversed(range(chunks)):
        halo_copy(c).start()

    lanes = lax.broadcasted_iota(jnp.int32, (1, width), 1) // head_size
    masks = [(lanes == h).astype(jnp.bfloat16) for h in range(HEADS)]
    picks = [lanes == h for h in range(HEADS - 1)]
    later = (
        lax.broadcasted_iota(jnp.int32, (HEADS * chunk, 128), 1)
        <= lax.broadcasted_iota(jnp.int32, (HEADS * chunk, 128), 0) % chunk
    )

    for load in loads[:2]:
        load.wait()

    group = 4

    def spread(src, start):
        def piece(i, carry):
            rows = normalized(src[pl.ds(start + i * 8, 8)].reshape(8 * ag_dev, width))
            wide[pl.ds(pl.multiple_of(i * 8 * ag_dev, 8 * ag_dev), 8 * ag_dev), :] = rows.astype(jnp.float32)
            return carry

        lax.fori_loop(0, chunk // 8, piece, 0)

    def project(row0, is_halo, start):
        def agents4(g, carry):
            parts = []
            for i in range(group):
                rows = wide[pl.ds(g * group + i, chunk, stride=ag_dev), :]
                parts.append(rows.astype(jnp.bfloat16))
            result = matmul(jnp.concatenate(parts, 0), wt[...])
            keys = result[:, width : 2 * width].astype(jnp.bfloat16)
            vals = result[:, 2 * width :].astype(jnp.bfloat16)
            at = pl.ds(g * group, group)
            k1[at, pl.ds(row0, chunk), :] = keys.reshape(group, chunk, width)
            v1[at, pl.ds(row0, chunk), :] = vals.reshape(group, chunk, width)
            if not is_halo:
                q1[at, pl.ds(start, chunk), :] = result[:, :width].astype(jnp.bfloat16).reshape(group, chunk, width)
            return carry

        lax.fori_loop(0, ag_dev // group, agents4, 0)

    extra = k1.shape[1] - 2 * tm_dev
    if extra:
        k1[:, pl.ds(2 * tm_dev, extra), :] = jnp.zeros((ag_dev, extra, width), jnp.bfloat16)
        v1[:, pl.ds(2 * tm_dev, extra), :] = jnp.zeros((ag_dev, extra, width), jnp.bfloat16)

    def own_chunk(c, carry):
        start = pl.multiple_of(c * chunk, chunk)
        spread(xv, start)
        project(pl.multiple_of(tm_dev + start, chunk), False, start)
        return carry

    lax.fori_loop(0, chunks, own_chunk, 0)
    for load in loads[2:]:
        load.wait()

    def mix_copies(k, p):
        start = (chunks - 1 - k) * chunk + p * part
        piece = k * PARTS + p
        away = pl.multiple_of(pair + core * ag_dev, ag_dev)
        result = []
        for i, (peer, target, slot) in enumerate(
            [(sibling, 1 - core, ag_dev), (far[0], 0, away), (far[1], 1, away)]
        ):
            result.append(
                pltpu.make_async_remote_copy(
                    src_ref=mixed.at[pl.ds(start + target * half, part)],
                    dst_ref=slab.at[pl.ds(piece * part, part), pl.ds(slot, ag_dev)],
                    send_sem=mix_send.at[piece, i],
                    recv_sem=mix_recv.at[piece, 0 if i == 0 else 1 + core],
                    device_id=peer, device_id_type=MESH,
                )
            )
        return result

    def mix_arrivals(piece):
        return [
            pltpu.make_async_remote_copy(
                src_ref=mixed.at[pl.ds(0, part)],
                dst_ref=slab.at[pl.ds(piece * part, part), pl.ds((i + 1) * ag_dev, ag_dev)],
                send_sem=mix_send.at[piece, i], recv_sem=mix_recv.at[piece, i],
                device_id=peer, device_id_type=MESH,
            )
            for i, peer in enumerate([sibling, far[0], far[1]])
        ]

    def temporal_chunk(k, carry):
        c = chunks - 1 - k
        start = pl.multiple_of(c * chunk, chunk)
        halo_copy(c).wait_recv()
        spread(halo, start)
        project(start, True, start)

        columns = lax.broadcasted_iota(jnp.int32, (1, WINDOW), 1) + start
        absent = jnp.where((tm == 0) & (columns < WINDOW), -1e30, 0.0)

        def temporal_agents(i, inner):
            ids = [i * UNROLL + j for j in range(UNROLL)]
            scores = [
                matmul(by_head(q1[a, pl.ds(start, chunk), :], masks), k1[a, pl.ds(start, WINDOW + 128), :], NT)
                for a in ids
            ]
            weights = []
            for score in scores:
                edge = jnp.where(later, score[:, WINDOW:], score[:, :128] + absent[:, :128])
                middle = score[:, 128:WINDOW] + absent[:, 128:]
                top = jnp.max(jnp.maximum(edge, middle), axis=1, keepdims=True)
                edge = jnp.exp2((edge - top) * factor)
                middle = jnp.exp2((middle - top) * factor)
                share = 1.0 / jnp.sum(edge + middle, axis=1, keepdims=True)
                edge = edge * share
                middle = middle * share
                weights.append(
                    jnp.concatenate(
                        [jnp.where(later, 0.0, edge), middle, jnp.where(later, edge, 0.0)], axis=1
                    ).astype(jnp.bfloat16)
                )
            sums = [matmul(weight, v1[a, pl.ds(start, WINDOW + 128), :]) for a, weight in zip(ids, weights)]
            attended = [pick_heads(value, chunk, picks).astype(jnp.bfloat16) for value in sums]
            update = matmul(jnp.concatenate(attended, 0), wto[...])
            for j, a in enumerate(ids):
                upd[pl.ds(a, chunk, stride=ag_dev), :] = update[j * chunk : (j + 1) * chunk]
            return inner

        lax.fori_loop(0, ag_dev // UNROLL, temporal_agents, 0)

        def add_piece(i, inner):
            rows = pl.ds(start + i * 8, 8)
            update = upd[pl.ds(pl.multiple_of(i * 8 * ag_dev, 8 * ag_dev), 8 * ag_dev), :]
            mixed[rows] = (xv[rows].astype(jnp.float32) + update.reshape(8, ag_dev, width)).astype(jnp.bfloat16)
            return inner

        lax.fori_loop(0, chunk // 8, add_piece, 0)
        slab[pl.ds(k * half, half), pl.ds(0, ag_dev), :] = mixed[pl.ds(start + core * half, half)]
        for p in range(PARTS):
            for copy in mix_copies(k, p):
                copy.start()
        return carry

    lax.fori_loop(0, chunks, temporal_chunk, 0)

    def result_copy(piece, owner):
        start = (chunks - 1 - piece // PARTS) * chunk + owner * half + piece % PARTS * part
        return pltpu.make_async_remote_copy(
            src_ref=sib_out.at[pl.ds(piece * part, part)], dst_ref=out_hbm.at[pl.ds(start, part)],
            send_sem=res_send.at[piece], recv_sem=res_recv.at[piece],
            device_id=sibling, device_id_type=MESH,
        )

    def store_copy(piece):
        start = (chunks - 1 - piece // PARTS) * chunk + core * half + piece % PARTS * part
        return pltpu.make_async_copy(
            own_out.at[pl.ds(piece * part, part)], out_hbm.at[pl.ds(start, part)], store_sem.at[piece]
        )

    blocks = lax.broadcasted_iota(jnp.int32, (1, width), 1) // pair
    none = jnp.zeros((agents, width), jnp.bfloat16)

    def cross_block(first):
        rows = slab[pl.ds(first, BLOCK)]
        normed = normalized(rows.reshape(BLOCK * agents, width))
        keys = matmul(normed, wc[:, width : 2 * width]).astype(jnp.bfloat16)
        values = matmul(wvt[...], normed, NT).astype(jnp.bfloat16)
        own = normed.reshape(BLOCK, agents, width)[:, :pair].reshape(BLOCK * pair, width)
        queries = matmul(own, wc[:, :width]).astype(jnp.bfloat16)
        weights = []
        for t in range(BLOCK):
            query = queries[t * pair : (t + 1) * pair]
            stacked = jnp.concatenate([query * masks[(place - t) % HEADS] for place in range(HEADS)], axis=0)
            scores = matmul(keys[t * agents : (t + 1) * agents], stacked, NT)
            powers = jnp.exp2((scores - jnp.max(scores, axis=0, keepdims=True)) * factor)
            share = 1.0 / jnp.sum(powers, axis=0, keepdims=True)
            weights.append((powers * share).astype(jnp.bfloat16))
        sums = []
        for t in range(0, BLOCK, 2):
            both = jnp.concatenate(
                [
                    jnp.concatenate([weights[t], none], axis=1),
                    jnp.concatenate([none, weights[t + 1]], axis=1),
                ],
                axis=0,
            )
            result = matmul(values[:, t * agents : (t + 2) * agents], both)
            sums += [result[:, :width], result[:, width:]]
        heads = []
        for h in range(HEADS):
            band = [value[h * head_size : (h + 1) * head_size] for value in sums]
            result = band[(HEADS - 1 - h) % HEADS]
            for place in range(HEADS - 1):
                result = jnp.where(blocks == place, band[(place - h) % HEADS], result)
            heads.append(pltpu.roll(result, width - h * pair, 1) if h else result)
        attended = jnp.concatenate(heads, axis=0).T.astype(jnp.bfloat16)
        update = matmul(attended, wco[...]).reshape(BLOCK, pair, width)
        final = (rows[:, :pair].astype(jnp.float32) + update).astype(jnp.bfloat16)
        own_out[pl.ds(first, BLOCK)] = final[:, :ag_dev]
        sib_out[pl.ds(first, BLOCK)] = final[:, ag_dev:]

    def cross_piece(piece, carry):
        for copy in mix_arrivals(piece):
            copy.wait_recv()

        def cross_blocks(i, inner):
            for j in range(BLOCKS):
                cross_block(piece * part + (i * BLOCKS + j) * BLOCK)
            return inner

        lax.fori_loop(0, part // (BLOCK * BLOCKS), cross_blocks, 0)
        result_copy(piece, core).start()
        store_copy(piece).start()
        return carry

    wvt[...] = wc[:, 2 * width :].astype(jnp.float32).T.astype(jnp.bfloat16)
    lax.fori_loop(0, pieces, cross_piece, 0)

    def drain(k, carry):
        halo_copy(k).wait_send()
        for p in range(PARTS):
            for copy in mix_copies(k, p):
                copy.wait_send()
            piece = k * PARTS + p
            result_copy(piece, core).wait_send()
            result_copy(piece, 1 - core).wait_recv()
            store_copy(piece).wait()
        return carry

    lax.fori_loop(0, chunks, drain, 0)


def local(panel, w_tqkv, w_tout, w_cqkv, w_cout):
    tm_dev, ag_dev, width = panel.shape
    chunk = 64
    chunks = tm_dev // chunk
    half = chunk // 2
    pieces = chunks * PARTS
    agents = ag_dev * lax.axis_size("agent")
    rows = WINDOW + tm_dev + (128 - chunk)
    bf16, f32 = jnp.bfloat16, jnp.float32
    any_spec = pl.BlockSpec(memory_space=pl.ANY)
    return pl.pallas_call(
        functools.partial(kernel, tm_axis="tm", agent_axis="agent", chunk=chunk),
        out_shape=jax.ShapeDtypeStruct(panel.shape, bf16),
        in_specs=[any_spec] * 5,
        out_specs=any_spec,
        scratch_shapes=[
            pltpu.VMEM(panel.shape, bf16),
            pltpu.VMEM(panel.shape, bf16),
            pltpu.VMEM(w_tqkv.shape, bf16),
            pltpu.VMEM(w_tout.shape, bf16),
            pltpu.VMEM(w_cqkv.shape, bf16),
            pltpu.VMEM(w_cout.shape, bf16),
            pltpu.VMEM((chunk * ag_dev, width), f32),
            pltpu.VMEM((ag_dev, tm_dev, width), bf16),
            pltpu.VMEM((ag_dev, rows, width), bf16),
            pltpu.VMEM((ag_dev, rows, width), bf16),
            pltpu.VMEM((chunk * ag_dev, width), f32),
            pltpu.VMEM(panel.shape, bf16),
            pltpu.VMEM((chunks * half, agents, width), bf16),
            pltpu.VMEM((width, width), bf16),
            pltpu.VMEM((chunks * half, ag_dev, width), bf16),
            pltpu.VMEM((chunks * half, ag_dev, width), bf16),
            pltpu.SemaphoreType.DMA((5,)),
            pltpu.SemaphoreType.DMA((chunks,)),
            pltpu.SemaphoreType.DMA((chunks,)),
            pltpu.SemaphoreType.DMA((pieces, 3)),
            pltpu.SemaphoreType.DMA((pieces, 3)),
            pltpu.SemaphoreType.DMA((pieces,)),
            pltpu.SemaphoreType.DMA((pieces,)),
            pltpu.SemaphoreType.DMA((pieces,)),
        ],
        compiler_params=pltpu.CompilerParams(
            collective_id=0, has_side_effects=True, vmem_limit_bytes=56 * 2**20
        ),
        name="axial_block",
    )(panel, w_tqkv, w_tout, w_cqkv, w_cout)


def solution(mesh):
    in_specs = (P("tm", "agent", None), P(), P(), P(), P())
    out_specs = P("tm", "agent", None)
    return jax.shard_map(local, mesh=mesh, in_specs=in_specs, out_specs=out_specs, check_vma=False)
```

time: 220 us -> 89.5 us (0.41)
  Pallas kernels: 0 us -> 87 us
  waiting for transfers between devices: 70 us -> 0 us
  matrix products: 61.7 us -> 0 us
  blocking collectives: 32.3 us -> 0 us
  local copies, waits for them, and re-layouts: 31.9 us -> 2.37 us
  starting transfers between devices: 12.7 us -> 0 us
  other arithmetic: 9.6 us -> 0 us
    pallas_call x0 -> x1, Pallas kernels: none -> 87 us  [local(): pl.pallas_call(functools.partial(kernel, tm_axis='tm', agent_axis='agent'...]
    ppermute x1 -> x0, waiting for transfers between devices: 41.4 us -> none  [shifted(): lax.ppermute(value, axis, [(source, source + steps) for source in range(l...]
    all_to_all x1 -> x0, blocking collectives: 32.3 us -> none  [local(): lax.all_to_all(result[None], 'agent', split_axis=2, concat_axis=0, tiled=...]
    dot_general x10 -> x0, matrix products: 32.1 us -> none  [the longest x2 15.9 us: temporal_group(): jnp.einsum('ahqk,kahe->qahe', weights, group_pairs[:, :, 1], preferred_el...]
    sub x6 -> x0, matrix products: 29.7 us -> none  [softmax_rows(): expo = jnp.exp(scores - top)]
    all_to_all x1 -> x0, waiting for transfers between devices: 28.7 us -> none  [local(): lax.all_to_all(blocks, 'agent', split_axis=0, concat_axis=2, tiled=True)[0]]
    all_to_all x1 -> x0, starting transfers between devices: 9.12 us -> none  [local(): lax.all_to_all(blocks, 'agent', split_axis=0, concat_axis=2, tiled=True)[0]]
    dynamic_slice x8 -> x0, local copies, waits for them, and re-layouts: 8.39 us -> none  [local(): across = lax.map(cross_block, grouped).reshape(slab.shape)]
  transfers between devices with their start and end apart: 2 -> 0, of which waited for: 2 -> 0; matrix products, arithmetic and copies ran while one was open for 2% -> 0% of each run, Pallas kernels for 0% -> 0%
where the time goes in v1:
time: 89.5 us; the launch traced here: 89.4 us
  Pallas kernels  87 us (97%)
  local copies, waits for them, and re-layouts  2.37 us (3%)
    pallas_call x1, Pallas kernels, local(): pl.pallas_call(functools.partial(kernel, tm_axis='tm', agent_axis='agent'...  87 us
    unnamed x1, local copies, waits for them, and re-layouts  2.37 us

profile of v1, /device:TPU:33, one launch (start us, length us, event | category | flops | bytes accessed | tf_op | source)
XLA Modules:
  0.0 89.4 jit_solution(14204778501407744734)
XLA Ops:
  0.0 87.0 %axial_block.1 = bf16[256,16,128]{2,1,0:T(8,128)(2,1)} custom-call(bf16[256,16,128]{2,1,0:T(8,128)(2,1)} %x_hbm.1, bf16[128,384]{1,0:T(8,128)(2,1)} %wt_hbm.1, bf16[128,128]{1,0:T(8,128)(2,1)} %wto_hbm.1, bf16[128,384]{1,0:T(8,128)(2,1)} %wc_hbm.1, bf16[128,128]{1,0:T(8,128)(2,1)} %wco_hbm.1), custom_call_target="tpu_custom_call" | custom-call | tf_op jit(solution)/shard_map/axial_block/pallas_call | solution.py:331
  87.0 2.4 %copy.7 = bf16[256,16,128]{2,1,0:T(8,128)(2,1)} copy(bf16[256,16,128]{2,1,0:T(8,128)(2,1)} %axial_block.1) | data formatting | bytes 2097152

commit v2 on v1

--- a/solution.py
+++ b/solution.py
@@ -14,7 +14,7 @@
 UNROLL = 4
 PARTS = 2
 BLOCK = 4
-BLOCKS = 2
+BLOCKS = 4
 MESH = pl.DeviceIdType.MESH
 NT = (((1,), (1,)), ((), ()))
 NN = (((1,), (0,)), ((), ()))
@@ -43,9 +43,9 @@
 
 
 def kernel(
-    x_hbm, wt_hbm, wto_hbm, wc_hbm, wco_hbm, out_hbm,
-    xv, halo, wt, wto, wc, wco, wide, q1, k1, v1, upd, mixed, slab, wvt, own_out, sib_out,
-    load_sem, halo_send, halo_recv, mix_send, mix_recv, res_send, res_recv, store_sem,
+    x_hbm, wt_hbm, wto_hbm, wc_hbm, wco_hbm, out,
+    xv, halo, wt, wto, wc, wco, wide, q1, k1, v1, upd, mixed, slab, wvt, sib_out,
+    load_sem, halo_send, halo_recv, mix_send, mix_recv, res_send, res_recv,
     *, tm_axis, agent_axis, chunk,
 ):
     tm_dev, ag_dev, width = xv.shape
@@ -234,35 +234,20 @@
     def result_copy(piece, owner):
         start = (chunks - 1 - piece // PARTS) * chunk + owner * half + piece % PARTS * part
         return pltpu.make_async_remote_copy(
-            src_ref=sib_out.at[pl.ds(piece * part, part)], dst_ref=out_hbm.at[pl.ds(start, part)],
+            src_ref=sib_out.at[pl.ds(piece * part, part)], dst_ref=out.at[pl.ds(start, part)],
             send_sem=res_send.at[piece], recv_sem=res_recv.at[piece],
             device_id=sibling, device_id_type=MESH,
         )
 
-    def store_copy(piece):
-        start = (chunks - 1 - piece // PARTS) * chunk + core * half + piece % PARTS * part
-        return pltpu.make_async_copy(
-            own_out.at[pl.ds(piece * part, part)], out_hbm.at[pl.ds(start, part)], store_sem.at[piece]
-        )
-
     blocks = lax.broadcasted_iota(jnp.int32, (1, width), 1) // pair
     none = jnp.zeros((agents, width), jnp.bfloat16)
 
-    def cross_block(first):
-        rows = slab[pl.ds(first, BLOCK)]
-        normed = normalized(rows.reshape(BLOCK * agents, width))
-        keys = matmul(normed, wc[:, width : 2 * width]).astype(jnp.bfloat16)
-        values = matmul(wvt[...], normed, NT).astype(jnp.bfloat16)
-        own = normed.reshape(BLOCK, agents, width)[:, :pair].reshape(BLOCK * pair, width)
-        queries = matmul(own, wc[:, :width]).astype(jnp.bfloat16)
-        weights = []
-        for t in range(BLOCK):
-            query = queries[t * pair : (t + 1) * pair]
-            stacked = jnp.concatenate([query * masks[(place - t) % HEADS] for place in range(HEADS)], axis=0)
-            scores = matmul(keys[t * agents : (t + 1) * agents], stacked, NT)
-            powers = jnp.exp2((scores - jnp.max(scores, axis=0, keepdims=True)) * factor)
-            share = 1.0 / jnp.sum(powers, axis=0, keepdims=True)
-            weights.append((powers * share).astype(jnp.bfloat16))
+    def softmax_columns(scores):
+        powers = jnp.exp2((scores - jnp.max(scores, axis=0, keepdims=True)) * factor)
+        share = 1.0 / jnp.sum(powers, axis=0, keepdims=True)
+        return (powers * share).astype(jnp.bfloat16)
+
+    def pair_sums(values, weights):
         sums = []
         for t in range(0, BLOCK, 2):
             both = jnp.concatenate(
@@ -274,6 +259,9 @@
             )
             result = matmul(values[:, t * agents : (t + 2) * agents], both)
             sums += [result[:, :width], result[:, width:]]
+        return sums
+
+    def gather_heads(sums):
         heads = []
         for h in range(HEADS):
             band = [value[h * head_size : (h + 1) * head_size] for value in sums]
@@ -281,24 +269,51 @@
             for place in range(HEADS - 1):
                 result = jnp.where(blocks == place, band[(place - h) % HEADS], result)
             heads.append(pltpu.roll(result, width - h * pair, 1) if h else result)
-        attended = jnp.concatenate(heads, axis=0).T.astype(jnp.bfloat16)
-        update = matmul(attended, wco[...]).reshape(BLOCK, pair, width)
-        final = (rows[:, :pair].astype(jnp.float32) + update).astype(jnp.bfloat16)
-        own_out[pl.ds(first, BLOCK)] = final[:, :ag_dev]
-        sib_out[pl.ds(first, BLOCK)] = final[:, ag_dev:]
+        return jnp.concatenate(heads, axis=0).T.astype(jnp.bfloat16)
+
+    def rotated_heads(query, t):
+        return jnp.concatenate([query * masks[(place - t) % HEADS] for place in range(HEADS)], axis=0)
+
+    def cross_group(firsts, target):
+        rows = [slab[pl.ds(first, BLOCK)] for first in firsts]
+        normed = [normalized(block.reshape(BLOCK * agents, width)) for block in rows]
+        keys = [matmul(block, wc[:, width : 2 * width]).astype(jnp.bfloat16) for block in normed]
+        own = [block.reshape(BLOCK, agents, width)[:, :pair].reshape(BLOCK * pair, width) for block in normed]
+        queries = [matmul(block, wc[:, :width]).astype(jnp.bfloat16) for block in own]
+        values = [matmul(wvt[...], block, NT).astype(jnp.bfloat16) for block in normed]
+        scores = [
+            [
+                matmul(
+                    key[t * agents : (t + 1) * agents],
+                    rotated_heads(query[t * pair : (t + 1) * pair], t),
+                    NT,
+                )
+                for t in range(BLOCK)
+            ]
+            for key, query in zip(keys, queries)
+        ]
+        weights = [[softmax_columns(score) for score in block] for block in scores]
+        sums = [pair_sums(value, weight) for value, weight in zip(values, weights)]
+        attended = [gather_heads(block) for block in sums]
+        update = matmul(jnp.concatenate(attended, axis=0), wco[...])
+        for j, first in enumerate(firsts):
+            added = update[j * BLOCK * pair : (j + 1) * BLOCK * pair].reshape(BLOCK, pair, width)
+            final = (rows[j][:, :pair].astype(jnp.float32) + added).astype(jnp.bfloat16)
+            out[pl.ds(target + j * BLOCK, BLOCK)] = final[:, :ag_dev]
+            sib_out[pl.ds(first, BLOCK)] = final[:, ag_dev:]
 
     def cross_piece(piece, carry):
         for copy in mix_arrivals(piece):
             copy.wait_recv()
 
+        start = (chunks - 1 - piece // PARTS) * chunk + core * half + piece % PARTS * part
+
         def cross_blocks(i, inner):
-            for j in range(BLOCKS):
-                cross_block(piece * part + (i * BLOCKS + j) * BLOCK)
+            cross_group([piece * part + (i * BLOCKS + j) * BLOCK for j in range(BLOCKS)], start + i * BLOCKS * BLOCK)
             return inner
 
         lax.fori_loop(0, part // (BLOCK * BLOCKS), cross_blocks, 0)
         result_copy(piece, core).start()
-        store_copy(piece).start()
         return carry
 
     wvt[...] = wc[:, 2 * width :].astype(jnp.float32).T.astype(jnp.bfloat16)
@@ -312,7 +327,6 @@
             piece = k * PARTS + p
             result_copy(piece, core).wait_send()
             result_copy(piece, 1 - core).wait_recv()
-            store_copy(piece).wait()
         return carry
 
     lax.fori_loop(0, chunks, drain, 0)
@@ -330,9 +344,9 @@
     any_spec = pl.BlockSpec(memory_space=pl.ANY)
     return pl.pallas_call(
         functools.partial(kernel, tm_axis="tm", agent_axis="agent", chunk=chunk),
-        out_shape=jax.ShapeDtypeStruct(panel.shape, bf16),
+        out_shape=pltpu.VMEM(panel.shape, bf16),
         in_specs=[any_spec] * 5,
-        out_specs=any_spec,
+        out_specs=pl.BlockSpec(memory_space=pltpu.VMEM),
         scratch_shapes=[
             pltpu.VMEM(panel.shape, bf16),
             pltpu.VMEM(panel.shape, bf16),
@@ -349,13 +363,11 @@
             pltpu.VMEM((chunks * half, agents, width), bf16),
             pltpu.VMEM((width, width), bf16),
             pltpu.VMEM((chunks * half, ag_dev, width), bf16),
-            pltpu.VMEM((chunks * half, ag_dev, width), bf16),
             pltpu.SemaphoreType.DMA((5,)),
             pltpu.SemaphoreType.DMA((chunks,)),
             pltpu.SemaphoreType.DMA((chunks,)),
             pltpu.SemaphoreType.DMA((pieces, 3)),
             pltpu.SemaphoreType.DMA((pieces, 3)),
-            pltpu.SemaphoreType.DMA((pieces,)),
             pltpu.SemaphoreType.DMA((pieces,)),
             pltpu.SemaphoreType.DMA((pieces,)),
         ],

time: 89.5 us -> 83.8 us (0.936)
  the two profiles are of different devices: /device:TPU:33 before, /device:TPU:1 now
where the time goes in v2:
time: 83.8 us; the launch traced here: 83.7 us
  Pallas kernels  82.7 us (99%)
  local copies, waits for them, and re-layouts  0.97 us (1%)
    pallas_call x1, Pallas kernels, local(): pl.pallas_call(functools.partial(kernel, tm_axis='tm', agent_axis='agent'...  82.7 us

profile of v2, /device:TPU:1, one launch (start us, length us, event | category | flops | bytes accessed | tf_op | source)
XLA Modules:
  0.0 83.7 jit_solution(15523279861569641235)
XLA Ops:
  0.0 82.7 %axial_block.1 = bf16[256,16,128]{2,1,0:T(8,128)(2,1)S(1)} custom-call(bf16[256,16,128]{2,1,0:T(8,128)(2,1)} %x_hbm.1, bf16[128,384]{1,0:T(8,128)(2,1)} %wt_hbm.1, bf16[128,128]{1,0:T(8,128)(2,1)} %wto_hbm.1, bf16[128,384]{1,0:T(8,128)(2,1)} %wc_hbm.1, bf16[128,128]{1,0:T(8,128)(2,1)} %wco_hbm.1), custom_call_target="tpu_custom_call" | custom-call | tf_op jit(solution)/shard_map/axial_block/pallas_call | solution.py:345
  82.7 1.0 %copy.7 = bf16[256,16,128]{2,1,0:T(8,128)(2,1)} copy(bf16[256,16,128]{2,1,0:T(8,128)(2,1)S(1)} %axial_block.1) | data formatting | bytes 2097152

commit v3 on v2

--- a/solution.py
+++ b/solution.py
@@ -77,9 +77,9 @@
         load.start()
 
     barrier = pltpu.get_barrier_semaphore()
-    for peer in (ahead, behind, sibling, far[0], far[1]):
+    for peer in (behind, sibling, far[0], far[1]):
         pl.semaphore_signal(barrier, inc=1, device_id=peer, device_id_type=MESH)
-    pl.semaphore_wait(barrier, 5)
+    pl.semaphore_wait(barrier, 4)
 
     def halo_copy(c):
         rows = pl.ds(c * chunk, chunk)
@@ -89,8 +89,17 @@
             device_id=ahead, device_id_type=MESH,
         )
 
-    for c in reversed(range(chunks)):
-        halo_copy(c).start()
+    has_ahead = tm < tm_count - 1
+    has_behind = tm > 0
+
+    @pl.when(has_ahead)
+    def _():
+        for c in reversed(range(chunks)):
+            halo_copy(c).start()
+
+    @pl.when(jnp.logical_not(has_behind))
+    def _():
+        halo[...] = jnp.zeros(halo.shape, halo.dtype)
 
     lanes = lax.broadcasted_iota(jnp.int32, (1, width), 1) // head_size
     masks = [(lanes == h).astype(jnp.bfloat16) for h in range(HEADS)]
@@ -179,7 +188,11 @@
     def temporal_chunk(k, carry):
         c = chunks - 1 - k
         start = pl.multiple_of(c * chunk, chunk)
-        halo_copy(c).wait_recv()
+
+        @pl.when(has_behind)
+        def _():
+            halo_copy(c).wait_recv()
+
         spread(halo, start)
         project(start, True, start)
 
@@ -320,7 +333,10 @@
     lax.fori_loop(0, pieces, cross_piece, 0)
 
     def drain(k, carry):
-        halo_copy(k).wait_send()
+        @pl.when(has_ahead)
+        def _():
+            halo_copy(k).wait_send()
+
         for p in range(PARTS):
             for copy in mix_copies(k, p):
                 copy.wait_send()

time: 83.8 us -> 81.9 us (0.977)
  the two profiles are of different devices: /device:TPU:1 before, /device:TPU:33 now
where the time goes in v3:
time: 81.9 us; the launch traced here: 81.8 us
  Pallas kernels  80.8 us (99%)
  local copies, waits for them, and re-layouts  0.97 us (1%)
    pallas_call x1, Pallas kernels, local(): pl.pallas_call(functools.partial(kernel, tm_axis='tm', agent_axis='agent'...  80.8 us

profile of v3, /device:TPU:33, one launch (start us, length us, event | category | flops | bytes accessed | tf_op | source)
XLA Modules:
  0.0 81.8 jit_solution(8543227305930535851)
XLA Ops:
  0.0 80.8 %axial_block.1 = bf16[256,16,128]{2,1,0:T(8,128)(2,1)S(1)} custom-call(bf16[256,16,128]{2,1,0:T(8,128)(2,1)} %x_hbm.1, bf16[128,384]{1,0:T(8,128)(2,1)} %wt_hbm.1, bf16[128,128]{1,0:T(8,128)(2,1)} %wto_hbm.1, bf16[128,384]{1,0:T(8,128)(2,1)} %wc_hbm.1, bf16[128,128]{1,0:T(8,128)(2,1)} %wco_hbm.1), custom_call_target="tpu_custom_call" | custom-call | tf_op jit(solution)/shard_map/axial_block/pallas_call | solution.py:361
  80.8 1.0 %copy.7 = bf16[256,16,128]{2,1,0:T(8,128)(2,1)} copy(bf16[256,16,128]{2,1,0:T(8,128)(2,1)S(1)} %axial_block.1) | data formatting | bytes 2097152
